TPU v7x, 1024 devices: a whole 4x4x32 slice. The times are simulated.
1024 devices in a mesh: pipe: 16 (over x, y_hi, core), expert: 64 (over z, y_lo).
Axes of the slice: x: 4, y: 4 (y_hi: 2, y_lo: 2; y = y_hi * 2 + y_lo), z: 32, core: 2. Of those that a mesh axis runs over, the one named last changes fastest.
Arguments:
- section_rows: bfloat16 [131072, 4096], P(('pipe', 'expert')), may hold values from -6 to 6
- route_ids: int32 [131072, 8], P(('pipe', 'expert')), may hold values from 0 to 127, as said below
- route_gates: bfloat16 [131072, 8], P(('pipe', 'expert')), may hold values from 0.099609375 to 1
- w_gate: bfloat16 [4096, 12288], P(None, 'expert'), may hold values from -0.09375 to 0.09375
- w_up: bfloat16 [4096, 12288], P(None, 'expert'), may hold values from -0.09375 to 0.09375
- w_down: bfloat16 [12288, 4096], P('expert'), may hold values from -0.15625 to 0.15625
Outputs:
- layer_out: bfloat16 [131072, 4096], P(('pipe', 'expert'))
Inputs may be any that keep to these rules, and one draw needn't show every extreme that they name: `route_ids`: each row names 8 different experts. In the rows of one device at most 4 name any one expert below 8, and on every relay rank one such expert is named by exactly 4 rows of every device.
All inputs are finite; a program needn't handle non-finite values.
Results may differ from a plain program's by a relative error of at most 0.0026.
Values may be sent and summed in bfloat16 or wider, within the bound.
A program may use at most 32 MiB of HBM per device.

v0:
```python
import jax
import jax.numpy as jnp
from jax import lax
from jax.sharding import PartitionSpec as P

GROUP = 8
CAP = 4


def from_behind(block, axis, distance):
    devices = range(lax.axis_size(axis))
    route = [((i - distance) % len(devices), i) for i in devices]
    return lax.ppermute(block, axis, route)


def expert_layer(rows, route_ids, route_gates, w_gate, w_up, w_down):
    tokens = rows.shape[0]
    width = rows.shape[1]
    devices = lax.axis_size("expert")
    e_win = devices // GROUP
    match = route_ids[:, :, None] == jnp.arange(e_win, dtype=jnp.int32)[None, None, :]
    hit = jnp.any(match, axis=1)
    weight = jnp.sum(jnp.where(match, route_gates.astype(jnp.float32)[:, :, None], 0.0), axis=1)
    place = jnp.cumsum(hit.astype(jnp.int32), axis=0) - 1
    slotted = hit[:, :, None] & (
        place[:, :, None] == jnp.arange(CAP, dtype=jnp.int32)[None, None, :]
    )
    slotted = slotted.reshape(tokens, e_win * CAP)
    packed = jnp.dot(
        slotted.astype(jnp.bfloat16).T, rows, preferred_element_type=jnp.float32
    ).astype(jnp.bfloat16)
    outgoing = jnp.repeat(packed.reshape(e_win, CAP, width), GROUP, axis=0)
    received = lax.all_to_all(outgoing, "expert", split_axis=0, concat_axis=0, tiled=True)
    count = received.shape[1]
    flat = received.reshape(devices * count, width)
    gate = jnp.dot(flat, w_gate, preferred_element_type=jnp.float32)
    upper = jnp.dot(flat, w_up, preferred_element_type=jnp.float32)
    hidden = (jax.nn.silu(gate) * upper).astype(jnp.bfloat16)
    partial_out = jnp.dot(hidden, w_down, preferred_element_type=jnp.float32).astype(jnp.bfloat16)
    partials = partial_out.reshape(devices, count, width)
    returned = lax.all_to_all(partials, "expert", split_axis=0, concat_axis=0, tiled=True)
    summed = jnp.sum(returned.astype(jnp.float32).reshape(e_win, GROUP, CAP, width), axis=1)
    weighted = slotted.astype(jnp.float32) * jnp.repeat(weight, CAP, axis=1)
    mixed = jnp.dot(weighted, summed.reshape(e_win * CAP, width), precision=lax.Precision.HIGHEST)
    return (rows.astype(jnp.float32) + mixed).astype(jnp.bfloat16)


def local(section_rows, route_ids, route_gates, w_gate, w_up, w_down):
    rows, gates = from_behind((section_rows, route_gates), "pipe", 1)
    named = from_behind(route_ids, "pipe", 1)
    return expert_layer(rows, named, gates, w_gate, w_up, w_down)


def solution(mesh):
    in_specs = (
        P(("pipe", "expert"), None),
        P(("pipe", "expert"), None),
        P(("pipe", "expert"), None),
        P(None, "expert"),
        P(None, "expert"),
        P("expert", None),
    )
    out_specs = P(("pipe", "expert"), None)
    return jax.shard_map(local, mesh=mesh, in_specs=in_specs, out_specs=out_specs, check_vma=False)
```

profile of v0, /device:TPU:24, one launch (start us, length us, event | category | flops | bytes accessed | tf_op | source)
XLA Modules:
  0.0 475.1 jit_solution(9682555570268039531)
XLA Ops:
  0.0 0.0 copy-start
  0.0 2.0 collective-permute-start
  2.1 4.2 collective-permute-start.1
  6.2 0.1 eq.46
  6.3 11.7 %collective-permute-done.1 = s32[128,8]{0,1:T(8,128)S(1)} collective-permute-done((s32[128,8]{0,1:T(8,128)}, s32[128,8]{0,1:T(8,128)S(1)}, u32[]{:S(2)}, u32[]{:S(2)}) %collective-permute-start.1) | collective-permute-done | bytes 4128 | tf_op jit(solution)/shard_map/ppermute | solution.py:13
  18.0 0.1 copy.20
  18.1 0.2 reduce_window_sum.11
  18.4 0.0 collective-permute-done
  18.4 0.0 copy-start.2
  18.4 0.9 copy-done.2
  19.3 0.3 convolution_convert_fusion.1
  19.7 0.1 reshape.42
  19.8 1.0 broadcast_in_dim.27
  20.8 228.4 %all_to_all.10 = bf16[64,4,4096]{2,1,0:T(4,128)(2,1)} all-to-all(bf16[64,4,4096]{2,1,0:T(4,128)(2,1)S(1)} %bitcast.17), channel_id=1, replica_groups=mesh['pipe'=16,'expert'=64] {'expert'}, dimensions={0} | all-to-all | bytes 4194304 | tf_op jit(solution)/shard_map/all_to_all | solution.py:33
  249.2 4.0 reshape.44
  253.2 0.0 copy-start.1
  253.2 3.0 fusion.22
  256.2 0.0 copy-done
  256.2 0.0 copy-done.1
  256.2 5.4 %convolution_convert_fusion = bf16[256,4096]{1,0:T(8,128)(2,1)} fusion(bf16[192,4096]{1,0:T(8,128)(2,1)S(1)} %copy-done, bf16[256,4096]{1,0:T(8,128)(2,1)} %reshape.44, bf16[4096,192]{0,1:T(8,128)(2,1)S(1)} %copy-done.1, f32[256,192]{0,1:T(8,128)S(1)} %fusion.22), kind=kOutput, calls=%fused_computation | convolution fusion | flops 806649856 | bytes 7536640 | tf_op jit(solution)/shard_map/dot_general | solution.py:39
  261.6 4.1 reshape.45
  265.8 0.0 copy-start.4
  265.8 5.6 %all-to-all-start.1 = ((bf16[64,4,4096]{2,1,0:T(4,128)(2,1)}), bf16[64,4,4096]{2,1,0:T(4,128)(2,1)}, u32[]{:S(2)}, u32[]{:S(2)}) async-start(bf16[64,4,4096]{2,1,0:T(4,128)(2,1)} %reshape.45), calls=%async_computation.1 | async-start | bytes 4194304 | tf_op jit(solution)/shard_map/all_to_all | solution.py:41
  271.4 0.0 copy-done.4
  271.4 0.0 copy-start.3
  271.4 2.1 collective-permute-start.2
  273.5 4.5 collective-permute-done.2
  278.0 191.5 %all-to-all-done.1 = bf16[64,4,4096]{2,1,0:T(4,128)(2,1)} async-done(((bf16[64,4,4096]{2,1,0:T(4,128)(2,1)}), bf16[64,4,4096]{2,1,0:T(4,128)(2,1)}, u32[]{:S(2)}, u32[]{:S(2)}) %all-to-all-start.1) | async-done | bytes 2097184 | tf_op jit(solution)/shard_map/all_to_all | solution.py:41
  469.4 2.7 convert_reduce_fusion
  472.2 0.0 copy-done.3
  472.2 2.9 add_convert_fusion
  (9 shorter events, 0.1 us)
Async XLA Ops:
  0.0 256.2 %copy-start = (bf16[192,4096]{1,0:T(8,128)(2,1)S(1)}, bf16[192,4096]{1,0:T(8,128)(2,1)}, u32[]{:S(2)}) copy-start(bf16[192,4096]{1,0:T(8,128)(2,1)} %param.11) | copy-start | bytes 4718596
  0.0 18.4 %collective-permute-start = (bf16[128,4096]{1,0:T(8,128)(2,1)}, bf16[128,4096]{1,0:T(8,128)(2,1)S(1)}, u32[]{:S(2)}, u32[]{:S(2)}) collective-permute-start(bf16[128,4096]{1,0:T(8,128)(2,1)} %param.6), channel_id=1, source_target_pairs={{960,0},{0,64},{64,128},{128,192},{192,256},{256,320},{320,384},{3... | collective-permute-start | bytes 3145736 | tf_op jit(solution)/shard_map/ppermute | solution.py:13
  2.1 15.9 %collective-permute-start.1 = (s32[128,8]{0,1:T(8,128)}, s32[128,8]{0,1:T(8,128)S(1)}, u32[]{:S(2)}, u32[]{:S(2)}) collective-permute-start(s32[128,8]{0,1:T(8,128)} %param.7), channel_id=1, source_target_pairs={{960,0},{0,64},{64,128},{128,192},{192,256},{256,320},{320,384},{3... | collective-permute-start | bytes 12296 | tf_op jit(solution)/shard_map/ppermute | solution.py:13
  18.4 1.0 copy-start.2
  253.2 3.0 copy-start.1
  265.8 5.6 %copy-start.4 = (bf16[128,8]{0,1:T(8,128)(2,1)S(1)}, bf16[128,8]{0,1:T(8,128)(2,1)}, u32[]{:S(2)}) copy-start(bf16[128,8]{0,1:T(8,128)(2,1)} %param.8) | copy-start | bytes 6148
  265.8 203.7 %all-to-all-start.1 = ((bf16[64,4,4096]{2,1,0:T(4,128)(2,1)}), bf16[64,4,4096]{2,1,0:T(4,128)(2,1)}, u32[]{:S(2)}, u32[]{:S(2)}) async-start(bf16[64,4,4096]{2,1,0:T(4,128)(2,1)} %reshape.45), calls=%async_computation.1 | async-start | bytes 4194304 | tf_op jit(solution)/shard_map/all_to_all | solution.py:41
  271.4 200.8 %copy-start.3 = (bf16[128,4096]{1,0:T(8,128)(2,1)S(1)}, bf16[128,4096]{1,0:T(8,128)(2,1)}, u32[]{:S(2)}) copy-start(bf16[128,4096]{1,0:T(8,128)(2,1)} %copy-done.2) | copy-start | bytes 3145732
  271.4 6.5 %collective-permute-start.2 = (bf16[128,8]{0,1:T(8,128)(2,1)S(1)}, bf16[128,8]{0,1:T(8,128)(2,1)S(1)}, u32[]{:S(2)}, u32[]{:S(2)}) collective-permute-start(bf16[128,8]{0,1:T(8,128)(2,1)S(1)} %copy-done.4), channel_id=1, source_target_pairs={{960,0},{0,64},{64,128},{128,192},{192,256},{256,320},{320,384},{3... | collective-permute-start | bytes 6152 | tf_op jit(solution)/shard_map/ppermute | solution.py:13
where the time goes:
time: 476 us; the launch traced here: 475 us
  blocking collectives  228 us (48%)
  waiting for transfers between devices  208 us (44%)
  starting transfers between devices  13.9 us (3%)
  matrix products  11.6 us (2%)
  local copies, waits for them, and re-layouts  10.4 us (2%)
    all_to_all x1, blocking collectives, expert_layer(): lax.all_to_all(outgoing, 'expert', split_axis=0, concat_axis=0, tiled=True)  228 us
    all_to_all x1, waiting for transfers between devices, expert_layer(): lax.all_to_all(partials, 'expert', split_axis=0, concat_axis=0, tiled=True)  191 us
    ppermute x3, waiting for transfers between devices, from_behind(): return lax.ppermute(block, axis, route)  16.2 us
  transfers between devices with their start and end apart: 4, of which 3 were waited for; matrix products, arithmetic and copies ran while one was open for 0% of the time, Pallas kernels for 0%

commit v1 on v0

v1 whole, which is shorter than its diff:
```python
import jax
import jax.numpy as jnp
from jax import lax
from jax.sharding import PartitionSpec as P

GROUP = 8
CAP = 4


def to_next(block, axis):
    n = lax.axis_size(axis)
    return lax.ppermute(block, axis, [(i, (i + 1) % n) for i in range(n)])


def routing(ids, gates, e_win):
    match = ids[:, :, None] == jnp.arange(e_win, dtype=jnp.int32)[None, None, :]
    hit = jnp.any(match, axis=1)
    weight = jnp.sum(jnp.where(match, gates.astype(jnp.float32)[:, :, None], 0.0), axis=1)
    place = jnp.cumsum(hit.astype(jnp.int32), axis=0) - 1
    slotted = hit[:, :, None] & (place[:, :, None] == jnp.arange(CAP, dtype=jnp.int32)[None, None, :])
    return slotted.reshape(ids.shape[0], e_win * CAP), weight


def local(section_rows, route_ids, route_gates, w_gate, w_up, w_down):
    devices = lax.axis_size("expert")
    e_win = devices // GROUP
    width = section_rows.shape[1]
    groups = [[g * GROUP + k for k in range(GROUP)] for g in range(e_win)]
    rows = to_next(section_rows, "pipe")
    slotted, weight = routing(route_ids, route_gates, e_win)
    packed = jnp.dot(slotted.astype(jnp.bfloat16).T, section_rows, preferred_element_type=jnp.float32).astype(jnp.bfloat16)
    half = CAP * width // GROUP
    outgoing = packed.reshape(e_win * GROUP, half)
    received = lax.all_to_all(outgoing, "expert", split_axis=0, concat_axis=0, tiled=True)
    gathered = lax.all_gather(received, "expert", axis_index_groups=groups, axis=0, tiled=False)
    flat = gathered.reshape(CAP, 2, devices, half).transpose(0, 2, 1, 3).reshape(CAP * devices, width)
    gate = jnp.dot(flat, w_gate, preferred_element_type=jnp.float32)
    upper = jnp.dot(flat, w_up, preferred_element_type=jnp.float32)
    hidden = (jax.nn.silu(gate) * upper).astype(jnp.bfloat16)
    partial_out = jnp.dot(hidden, w_down, preferred_element_type=jnp.float32).astype(jnp.bfloat16)
    pieces = partial_out.reshape(CAP, devices, 2, half).transpose(0, 2, 1, 3).reshape(GROUP, devices * half)
    spread = lax.all_to_all(pieces, "expert", split_axis=0, concat_axis=0, axis_index_groups=groups, tiled=True)
    summed = jnp.sum(spread.astype(jnp.float32), axis=0).astype(jnp.bfloat16).reshape(devices, half)
    returned = lax.all_to_all(summed, "expert", split_axis=0, concat_axis=0, tiled=True)
    returned = to_next(returned.reshape(e_win * CAP, width), "pipe")
    weighted = (slotted.astype(jnp.float32) * jnp.repeat(weight, CAP, axis=1)).astype(jnp.bfloat16)
    weighted = to_next(weighted, "pipe")
    mixed = jnp.dot(weighted, returned, preferred_element_type=jnp.float32)
    return (rows.astype(jnp.float32) + mixed).astype(jnp.bfloat16)


def solution(mesh):
    in_specs = (
        P(("pipe", "expert"), None),
        P(("pipe", "expert"), None),
        P(("pipe", "expert"), None),
        P(None, "expert"),
        P(None, "expert"),
        P("expert", None),
    )
    out_specs = P(("pipe", "expert"), None)
    return jax.shard_map(local, mesh=mesh, in_specs=in_specs, out_specs=out_specs, check_vma=False)
```

time: 476 us -> 343 us (0.72)
  the two profiles are of different devices: /device:TPU:24 before, /device:TPU:8 now
where the time goes in v1:
time: 343 us; the launch traced here: 342 us
  blocking collectives  125 us (36%)
  waiting for transfers between devices  94.7 us (28%)
  local copies, waits for them, and re-layouts  37.1 us (11%)
  starting transfers between devices  31.9 us (9%)
  other arithmetic  28.9 us (8%)
  between operations  13.6 us (4%)
  matrix products  10.5 us (3%)
    all_to_all x1, blocking collectives, local(): lax.all_to_all(outgoing, 'expert', split_axis=0, concat_axis=0, tiled=True)  72.5 us
    all_to_all x1, blocking collectives, local(): lax.all_to_all(pieces, 'expert', split_axis=0, concat_axis=0, axis_index_...  52.7 us
    all_gather x1, waiting for transfers between devices, local(): lax.all_gather(received, 'expert', axis_index_groups=groups, axis=0, tile...  50.8 us
    all_to_all x1, waiting for transfers between devices, local(): lax.all_to_all(summed, 'expert', split_axis=0, concat_axis=0, tiled=True)  39.1 us
    all_to_all x1, starting transfers between devices, local(): lax.all_to_all(summed, 'expert', split_axis=0, concat_axis=0, tiled=True)  23.4 us
    unnamed x17, local copies, waits for them, and re-layouts  15.3 us
    all_to_all x1, other arithmetic, local(): lax.all_to_all(pieces, 'expert', split_axis=0, concat_axis=0, axis_index_...  14.3 us
    ppermute x3, starting transfers between devices, to_next(): return lax.ppermute(block, axis, [(i, (i + 1) % n) for i in range(n)])  8.5 us
  transfers between devices with their start and end apart: 5, of which 3 were waited for; matrix products, arithmetic and copies ran while one was open for 1% of the time, Pallas kernels for 0%

profile of v1, /device:TPU:8, one launch (start us, length us, event | category | flops | bytes accessed | tf_op | source)
XLA Modules:
  0.0 341.8 jit_solution(11944152403774513819)
XLA Ops:
  6.5 0.8 fusion.7
  7.7 0.7 convert_element_type.34
  8.4 0.7 select_reduce_fusion
  9.3 1.5 convolution_convert_fusion.1
  11.3 0.5 broadcast.24
  11.8 2.1 reduce.3
  14.1 72.5 %all_to_all.30 = bf16[64,2,1024]{2,1,0:T(2,128)(2,1)S(1)} all-to-all(bf16[64,2,1024]{2,1,0:T(2,128)(2,1)S(1)} %reshape.53), channel_id=1, replica_groups=mesh['pipe'=16,'expert'=64] {'expert'}, dimensions={0} | all-to-all | bytes 524288 | tf_op jit(solution)/shard_map/all_to_all | solution.py:34
  86.8 0.9 copy.33
  87.7 50.8 %all-gather.3.cloned.1.call-done = bf16[512,1,2048]{2,0,1:T(8,128)(2,1)} async-done(((bf16[64,1,2048]{2,0,1:T(8,128)(2,1)}), bf16[512,1,2048]{2,0,1:T(8,128)(2,1)}) %all-gather.3.cloned.1.call-update) | async-done | bytes 2097168 | tf_op jit(solution)/shard_map/all_gather | solution.py:35
  138.4 3.7 %copy.34 = bf16[4,64,2,2048]{3,2,1,0:T(2,128)(2,1)S(1)} copy(bf16[4,64,2,2048]{3,1,2,0:T(8,128)(2,1)} %bitcast.27) | data formatting | bytes 4194304 | tf_op jit(solution)/shard_map/transpose | solution.py:36
  142.2 0.9 copy.38
  143.1 1.3 copy-done.1
  144.4 0.8 fusion.9
  145.3 5.5 %convolution_convert_fusion = bf16[256,4096]{1,0:T(8,128)(2,1)} fusion(bf16[192,4096]{1,0:T(8,128)(2,1)S(1)} %copy-done, bf16[256,4096]{1,0:T(8,128)(2,1)} %bitcast.24, bf16[4096,192]{0,1:T(8,128)(2,1)S(1)} %copy-done.2, f32[256,192]{0,1:T(8,128)S(1)} %fusion.9), kind=kOutput, calls=%fused_computation | convolution fusion | flops 806649856 | bytes 7536640 | tf_op jit(solution)/shard_map/dot_general | solution.py:40
  150.8 4.5 %reshape.48 = bf16[4,64,2,2048]{3,2,1,0:T(2,128)(2,1)} reshape(bf16[256,4096]{1,0:T(8,128)(2,1)} %convolution_convert_fusion) | data formatting | bytes 4194304 | tf_op jit(solution)/shard_map/reshape | solution.py:41
  155.3 3.8 %copy.40 = bf16[4,64,2,2048]{3,1,2,0:T(8,128)(2,1)} copy(bf16[4,64,2,2048]{3,2,1,0:T(2,128)(2,1)} %reshape.48) | data formatting | bytes 4194304 | tf_op jit(solution)/shard_map/reshape | solution.py:41
  159.1 7.4 %all_to_all.25 = bf16[8,1,131072]{2,1,0:T(2,128)(2,1)} reshape(bf16[4,2,64,2048]{3,2,1,0:T(8,128)(2,1)} %bitcast.25) | data formatting | bytes 4194304 | tf_op jit(solution)/shard_map/all_to_all | solution.py:42
  166.5 14.3 %reduce.4 = bf16[8,131072]{1,0:T(8,128)(2,1)} reduce(bf16[8,1,131072]{2,1,0:T(2,128)(2,1)} %all_to_all.25, bf16[]{:T(256)} %broadcast.24), dimensions={1}, to_apply=%all_to_all.25.reduce_sub_computation | reduce | bytes 4194306 | tf_op jit(solution)/shard_map/all_to_all | solution.py:42
  180.8 4.8 %reshape.55 = bf16[8,2,65536]{2,1,0:T(2,128)(2,1)} reshape(bf16[8,131072]{1,0:T(8,128)(2,1)} %reduce.4) | data formatting | bytes 4194304
  185.6 52.7 %all_to_all.31 = bf16[8,2,65536]{2,1,0:T(2,128)(2,1)} all-to-all(bf16[8,2,65536]{2,1,0:T(2,128)(2,1)} %reshape.55), channel_id=1, replica_groups={{0,1,2,3,4,5,6,7},{8,9,10,11,12,13,14,15},{16,17,18,19,20,21,22,23},{24..., dimensions={0} | all-to-all | bytes 4194304 | tf_op jit(solution)/shard_map/all_to_all | solution.py:42
  238.3 6.8 %reshape.56 = bf16[8,1,131072]{2,1,0:T(2,128)(2,1)} reshape(bf16[8,2,65536]{2,1,0:T(2,128)(2,1)} %all_to_all.31) | data formatting | bytes 4194304
  245.1 6.4 %reduce_sum.22 = bf16[131072]{0:T(1024)(128)(2,1)S(1)} reduce(bf16[8,1,131072]{2,1,0:T(2,128)(2,1)} %reshape.56, bf16[]{:T(256)} %constant.16.clone.1), dimensions={0,1}, to_apply=%region_3.4 | reduce | flops 917504 | bytes 2359298 | tf_op jit(solution)/shard_map/reduce_sum | solution.py:43
  251.6 2.2 reduce.5
  253.8 0.9 reshape.57
  254.6 23.4 %all-to-all-start.2 = ((bf16[64,2,1024]{2,1,0:T(2,128)(2,1)}), bf16[64,2,1024]{2,1,0:T(2,128)(2,1)S(1)}, u32[]{:S(2)}, u32[]{:S(2)}) async-start(bf16[64,2,1024]{2,1,0:T(2,128)(2,1)} %reshape.57), calls=%async_computation.2 | async-start | bytes 524288 | tf_op jit(solution)/shard_map/all_to_all | solution.py:44
  278.0 1.9 collective-permute-start
  280.0 39.1 %all-to-all-done.2 = bf16[64,2,1024]{2,1,0:T(2,128)(2,1)S(1)} async-done(((bf16[64,2,1024]{2,1,0:T(2,128)(2,1)}), bf16[64,2,1024]{2,1,0:T(2,128)(2,1)S(1)}, u32[]{:S(2)}, u32[]{:S(2)}) %all-to-all-start.2) | async-done | bytes 262176 | tf_op jit(solution)/shard_map/all_to_all | solution.py:44
  319.3 1.5 reduce.2
  320.9 1.9 collective-permute-start.2
  322.8 4.7 %collective-permute-start.1 = (bf16[128,32]{0,1:T(8,128)(2,1)S(1)}, bf16[128,32]{0,1:T(8,128)(2,1)S(1)}, u32[]{:S(2)}, u32[]{:S(2)}) collective-permute-start(bf16[128,32]{0,1:T(8,128)(2,1)S(1)} %get-tuple-element.5), channel_id=1, source_target_pairs={{0,64},{64,128},{128,192},{192,256},{256,320},{320,384},{384,448},... | collective-permute-start | bytes 24584 | tf_op jit(solution)/shard_map/ppermute | solution.py:12
  327.5 4.8 %collective-permute-done.1 = bf16[128,32]{0,1:T(8,128)(2,1)S(1)} collective-permute-done((bf16[128,32]{0,1:T(8,128)(2,1)S(1)}, bf16[128,32]{0,1:T(8,128)(2,1)S(1)}, u32[]{:S(2)}, u32[]{:S(2)}) %collective-permute-start.1) | collective-permute-done | bytes 8224 | tf_op jit(solution)/shard_map/ppermute | solution.py:12
  332.3 2.7 add_convert_fusion
  (30 shorter events, 1.9 us)
Async XLA Ops:
  6.5 138.7 %copy-start = (bf16[192,4096]{1,0:T(8,128)(2,1)S(1)}, bf16[192,4096]{1,0:T(8,128)(2,1)}, u32[]{:S(2)}) copy-start(bf16[192,4096]{1,0:T(8,128)(2,1)} %param.11) | copy-start | bytes 4718596
  6.5 131.9 %all-gather.3.cloned.1.call-start = ((), (), s32[]{:S(2)}) async-start(), calls=%async_computation.3 | async-start | bytes 2359296 | tf_op jit(solution)/shard_map/all_gather | solution.py:35
  142.2 2.2 copy-start.3
  143.1 1.3 copy-start.1
  143.1 2.2 copy-start.2
  251.4 26.6 %copy-start.4 = (bf16[128,4096]{1,0:T(8,128)(2,1)S(1)}, bf16[128,4096]{1,0:T(8,128)(2,1)}, u32[]{:S(2)}) copy-start(bf16[128,4096]{1,0:T(8,128)(2,1)} %param.6) | copy-start | bytes 3145732
  254.6 64.4 %all-to-all-start.2 = ((bf16[64,2,1024]{2,1,0:T(2,128)(2,1)}), bf16[64,2,1024]{2,1,0:T(2,128)(2,1)S(1)}, u32[]{:S(2)}, u32[]{:S(2)}) async-start(bf16[64,2,1024]{2,1,0:T(2,128)(2,1)} %reshape.57), calls=%async_computation.2 | async-start | bytes 524288 | tf_op jit(solution)/shard_map/all_to_all | solution.py:44
  278.0 54.2 %collective-permute-start = (bf16[128,4096]{1,0:T(8,128)(2,1)S(1)}, bf16[128,4096]{1,0:T(8,128)(2,1)}, u32[]{:S(2)}, u32[]{:S(2)}) collective-permute-start(bf16[128,4096]{1,0:T(8,128)(2,1)S(1)} %copy-done.4), channel_id=1, source_target_pairs={{0,64},{64,128},{128,192},{192,256},{256,320},{320,384},{384,448},... | collective-permute-start | bytes 3145736 | tf_op jit(solution)/shard_map/ppermute | solution.py:12
  320.9 11.4 %collective-permute-start.2 = (bf16[32,4096]{1,0:T(8,128)(2,1)S(1)}, bf16[32,4096]{1,0:T(8,128)(2,1)S(1)}, u32[]{:S(2)}, u32[]{:S(2)}) collective-permute-start(bf16[32,4096]{1,0:T(8,128)(2,1)S(1)} %reshape.49), channel_id=1, source_target_pairs={{0,64},{64,128},{128,192},{192,256},{256,320},{320,384},{384,448},... | collective-permute-start | bytes 786440 | tf_op jit(solution)/shard_map/ppermute | solution.py:12
  322.8 9.5 %collective-permute-start.1 = (bf16[128,32]{0,1:T(8,128)(2,1)S(1)}, bf16[128,32]{0,1:T(8,128)(2,1)S(1)}, u32[]{:S(2)}, u32[]{:S(2)}) collective-permute-start(bf16[128,32]{0,1:T(8,128)(2,1)S(1)} %get-tuple-element.5), channel_id=1, source_target_pairs={{0,64},{64,128},{128,192},{192,256},{256,320},{320,384},{384,448},... | collective-permute-start | bytes 24584 | tf_op jit(solution)/shard_map/ppermute | solution.py:12
Sparse Core Ops, SparseCore 0:
  87.8 50.6 all-gather.2
